TPU v7x, 512 devices: a whole 4x8x8 slice. The times are simulated.
512 devices in a mesh: dp: 8 (over x, core), ctx: 64 (over y, z).
Axes of the slice: x: 4, y: 8, z: 8, core: 2. Of those that a mesh axis runs over, the one named last changes fastest.
Arguments:
- queries: bfloat16 [8192, 4096], P(('dp', 'ctx')), may hold values from -150 to 150
- keys: bfloat16 [131072, 1024], P(('dp', 'ctx')), may hold values from -8 to 8
- values: bfloat16 [131072, 1024], P(('dp', 'ctx')), may hold values from -6 to 6
- learned_compress_queries: bfloat16 [16, 1024], replicated, may hold values from -150 to 150
- span_len: int32 [8, 64], P('dp', 'ctx'), may hold values from 1 to 16, 768 in all within a row
- span_offset: int32 [8, 64], P('dp', 'ctx'), may hold values from 0 to 240
- destination: int32 [8192, 1], P(('dp', 'ctx')), may hold values from 0 to 63; in each aligned block of 16 rows (0 to 15, 16 to 31, ...) at most 2 rows name the same one
- cotangent: bfloat16 [8192, 4096], P(('dp', 'ctx')), may hold values from -6 to 6
- adapter_a: bfloat16 [64, 16, 4096], P('ctx'), may hold values from -0.09375 to 0.09375
- adapter_b: bfloat16 [64, 16, 4096], P('ctx'), may hold values from -0.09375 to 0.09375
Outputs:
- grad_rows: bfloat16 [8192, 4096], P(('dp', 'ctx'))
- grad_a: float32 [64, 16, 4096], P('ctx')
- grad_b: float32 [64, 16, 4096], P('ctx')
Inputs may be any that keep to these rules, and one draw needn't show every extreme that they name: `destination`: in each device's 16 slots (aligned blocks of rows) no decoder is named more than 2 times, a bound that some block reaches.
All inputs are finite; a program needn't handle non-finite values. No bound on the sum of `span_len` on one device may be relied on, other than what follows from the above.
Results may differ from a plain program's by a relative error of at most 0.025.
Values may be sent and summed in bfloat16 or wider, within the bound.
A program may use at most 64 MiB of HBM per device.

v0:
```python
import math
import jax
import jax.numpy as jnp
from jax import lax
from jax.sharding import PartitionSpec as P

QUERY_HEADS = 32
KEY_VALUE_HEADS = 8
HEAD_SIZE = 128
COMPRESSED_ROWS = 16
SCALE = 2.0
EPS = 1e-06
NEGATIVE_FLOOR = -1e30


def absorb(state, query_matrix, keys_blk, vals_blk, visible):
    count = keys_blk.shape[0]
    heads = query_matrix.shape[1]
    width = query_matrix.shape[3]
    expanded_keys = keys_blk.reshape(count, heads, width)
    expanded_values = vals_blk.reshape(count, heads, width)
    attention_score = jnp.einsum(
        "shgd,nhd->shgn", query_matrix, expanded_keys, preferred_element_type=jnp.float32
    ) * (1.0 / math.sqrt(width))
    seen = visible[:, None, None, :]
    attention_score = jnp.where(seen, attention_score, NEGATIVE_FLOOR)
    peak, total, accum = state
    newpeak = jnp.maximum(peak, jnp.max(attention_score, axis=-1))
    keep = jnp.exp(peak - newpeak)
    prob = jnp.where(seen, jnp.exp(attention_score - newpeak[..., None]), 0.0)
    total = total * keep + jnp.sum(prob, axis=-1)
    accum = accum * keep[..., None] + jnp.einsum(
        "shgn,nhd->shgd",
        prob.astype(jnp.bfloat16),
        expanded_values,
        preferred_element_type=jnp.float32,
    )
    return (newpeak, total, accum)


def absorb_rows(state, query_matrix, keys_blk, vals_blk, visible):
    count = keys_blk.shape[0]
    blocks = count // 256
    kb = keys_blk.reshape(blocks, 256, keys_blk.shape[1])
    vb = vals_blk.reshape(blocks, 256, vals_blk.shape[1])
    mb = visible.reshape(visible.shape[0], blocks, 256).transpose(1, 0, 2)

    def step(current, item):
        return (absorb(current, query_matrix, item[0], item[1], item[2]), None)

    state, _ = lax.scan(step, state, (kb, vb, mb))
    return state


def attend(queries, keys, values, learned_compress_queries, offset, length):
    span_slots = queries.shape[0]
    model = queries.shape[1]
    segment_length = keys.shape[0]
    query_group = QUERY_HEADS // KEY_VALUE_HEADS
    here = lax.axis_index("ctx")
    query_matrix = queries.reshape(span_slots, KEY_VALUE_HEADS, query_group, HEAD_SIZE)
    expanded_keys = keys.reshape(segment_length, KEY_VALUE_HEADS, HEAD_SIZE)
    expanded_values = values.reshape(segment_length, KEY_VALUE_HEADS, HEAD_SIZE)
    compressor_query = learned_compress_queries.reshape(COMPRESSED_ROWS, KEY_VALUE_HEADS, HEAD_SIZE)
    attention_score = jnp.einsum(
        "cpf,ipf->pci", compressor_query, expanded_keys, preferred_element_type=jnp.float32
    ) * (1.0 / math.sqrt(HEAD_SIZE))
    softmax_weight = jax.nn.softmax(attention_score, axis=-1).astype(jnp.bfloat16)
    short_keys = (
        jnp.einsum(
            "wio,owx->iwx", softmax_weight, expanded_keys, preferred_element_type=jnp.float32
        )
        .astype(jnp.bfloat16)
        .reshape(COMPRESSED_ROWS, KEY_VALUE_HEADS * HEAD_SIZE)
    )
    short_vals = (
        jnp.einsum(
            "wio,owx->iwx", softmax_weight, expanded_values, preferred_element_type=jnp.float32
        )
        .astype(jnp.bfloat16)
        .reshape(COMPRESSED_ROWS, KEY_VALUE_HEADS * HEAD_SIZE)
    )
    state = (
        jnp.full((span_slots, KEY_VALUE_HEADS, query_group), NEGATIVE_FLOOR, jnp.float32),
        jnp.zeros((span_slots, KEY_VALUE_HEADS, query_group), jnp.float32),
        jnp.zeros((span_slots, KEY_VALUE_HEADS, query_group, HEAD_SIZE), jnp.float32),
    )
    position = offset + jnp.arange(span_slots, dtype=jnp.int32)
    local = jnp.arange(segment_length, dtype=jnp.int32)[None, :] <= position[:, None]
    state = absorb(state, query_matrix, keys, values, local)
    piece = (
        lax.all_gather(short_keys, "ctx", axis=0, tiled=True),
        lax.all_gather(short_vals, "ctx", axis=0, tiled=True),
    )
    count = piece[0].shape[0]
    source = jnp.arange(count, dtype=jnp.int32) // COMPRESSED_ROWS
    state = absorb_rows(state, query_matrix, piece[0], piece[1], (source < here)[None, :])
    peak, total, accum = state
    out = (accum / total[..., None]).reshape(span_slots, model)
    live = (jnp.arange(span_slots, dtype=jnp.int32) < length)[:, None]
    return jnp.where(live, out, 0.0).astype(jnp.bfloat16)


def shards(
    queries,
    keys,
    values,
    learned_compress_queries,
    span_len,
    span_offset,
    destination,
    cotangent,
    adapter_a,
    adapter_b,
):
    span_slots = queries.shape[0]
    model = queries.shape[1]
    count = lax.axis_size("ctx")
    cap = max(2, (3 * span_slots + 2 * count - 1) // (2 * count))
    offset = span_offset[0, 0]
    length = span_len[0, 0]
    live = (jnp.arange(span_slots, dtype=jnp.int32) < length)[:, None]
    dy = jnp.where(live, cotangent, jnp.zeros_like(cotangent))
    target = destination[:, 0]
    order_idx = jnp.arange(span_slots, dtype=jnp.int32)
    same = target[:, None] == target[None, :]
    before = order_idx[None, :] < order_idx[:, None]
    rank = jnp.sum((same & before).astype(jnp.int32), axis=1)
    slot = target * cap + rank
    place = (jnp.arange(count * cap, dtype=jnp.int32)[:, None] == slot[None, :]).astype(
        jnp.bfloat16
    )

    def packed(row_block):
        return (
            jnp.dot(place, row_block, preferred_element_type=jnp.float32)
            .astype(jnp.bfloat16)
            .reshape(count, cap, model)
        )

    attn = attend(queries, keys, values, learned_compress_queries, offset, length)
    rows_in, dy_in = (
        lax.all_to_all(packed(attn), "ctx", split_axis=0, concat_axis=0, tiled=True),
        lax.all_to_all(packed(dy), "ctx", split_axis=0, concat_axis=0, tiled=True),
    )
    x = rows_in.reshape(count * cap, model).astype(jnp.float32)
    grads_in = dy_in.reshape(count * cap, model)
    rs = lax.rsqrt(jnp.mean(x * x, axis=-1, keepdims=True) + EPS)
    nrm = x * rs
    normed = nrm.astype(jnp.bfloat16)
    down = adapter_a[0]
    upper = adapter_b[0]
    across = (((1,), (1,)), ((), ()))
    along = (((0,), (0,)), ((), ()))
    hid = lax.dot_general(normed, down, across, preferred_element_type=jnp.float32).astype(
        jnp.bfloat16
    )
    back = (
        SCALE * lax.dot_general(grads_in, upper, across, preferred_element_type=jnp.float32)
    ).astype(jnp.bfloat16)
    grad_b = SCALE * lax.dot_general(hid, grads_in, along, preferred_element_type=jnp.float32)
    grad_a = lax.dot_general(back, normed, along, preferred_element_type=jnp.float32)
    dn = jnp.dot(back, down, preferred_element_type=jnp.float32)
    d_rows = (
        grads_in.astype(jnp.float32) + rs * (dn - nrm * jnp.mean(dn * nrm, axis=-1, keepdims=True))
    ).astype(jnp.bfloat16)
    returned = lax.all_to_all(
        d_rows.reshape(count, cap, model), "ctx", split_axis=0, concat_axis=0, tiled=True
    )
    grad_rows = lax.dot_general(
        place, returned.reshape(count * cap, model), along, preferred_element_type=jnp.float32
    ).astype(jnp.bfloat16)
    grad_a, grad_b = (
        lax.psum(grad_a.astype(jnp.bfloat16), "dp").astype(jnp.float32),
        lax.psum(grad_b.astype(jnp.bfloat16), "dp").astype(jnp.float32),
    )
    return (grad_rows, grad_a[None], grad_b[None])


def solution(mesh):
    in_specs = (
        P(("dp", "ctx"), None),
        P(("dp", "ctx"), None),
        P(("dp", "ctx"), None),
        P(),
        P("dp", "ctx"),
        P("dp", "ctx"),
        P(("dp", "ctx"), None),
        P(("dp", "ctx"), None),
        P("ctx", None, None),
        P("ctx", None, None),
    )
    out_specs = (P(("dp", "ctx"), None), P("ctx", None, None), P("ctx", None, None))
    return jax.shard_map(shards, mesh=mesh, in_specs=in_specs, out_specs=out_specs, check_vma=False)
```

profile of v0, /device:TPU:8, one launch (start us, length us, event | category | flops | bytes accessed | tf_op | source)
XLA Modules:
  0.0 355.6 jit_solution(18318135870249494899)
XLA Ops:
  7.2 1.5 fusion.61
  8.8 1.3 fusion.19
  10.1 0.6 copy.103
  10.8 1.3 fusion.20
  12.0 0.6 copy.102
  13.4 0.2 convert_reduce_fusion
  13.6 0.5 convolution_convert_fusion.1
  14.1 1.5 reshape.203
  15.6 16.9 %all-to-all-start = ((bf16[64,2,4096]{2,1,0:T(2,128)(2,1)}), bf16[64,2,4096]{2,1,0:T(2,128)(2,1)}, u32[]{:S(2)}, u32[]{:S(2)}) async-start(bf16[64,2,4096]{2,1,0:T(2,128)(2,1)} %reshape.203), calls=%async_computation | async-start | bytes 2097152 | tf_op jit(solution)/shard_map/all_to_all | solution.py:144
  33.6 0.4 fusion.60
  34.0 0.3 fusion.32
  34.3 0.3 fusion.16
  34.6 82.2 %all-gather.3.cloned.1.call-done = bf16[1024,1024]{1,0:T(8,128)(2,1)} async-done(((bf16[16,1024]{1,0:T(8,128)(2,1)}), bf16[1024,1024]{1,0:T(8,128)(2,1)}) %all-gather.3.cloned.1.call-update) | async-done | bytes 2097168 | tf_op jit(solution)/shard_map/all_gather | solution.py:92
  116.9 84.1 %all-gather.5.cloned.1.call-done = bf16[1024,1024]{1,0:T(8,128)(2,1)} async-done(((bf16[16,1024]{1,0:T(8,128)(2,1)}), bf16[1024,1024]{1,0:T(8,128)(2,1)}) %all-gather.5.cloned.1.call-update) | async-done | bytes 2097168 | tf_op jit(solution)/shard_map/all_gather | solution.py:93
  201.0 11.0 %while.14 = (s32[]{:T(128)}, f32[16,8,4]{0,2,1:T(4,128)S(1)}, f32[16,8,4]{0,2,1:T(4,128)S(1)}, f32[16,8,4,128]{3,0,2,1:T(8,128)S(1)}, pred[4,1,256]{2,1,0:T(4,12...) while((s32[]{:T(128)}, f32[16,8,4]{0,2,1:T(4,128)S(1)}, ...), condition=%wide.region_8.9_spmd, body=%wide.region_5.8_spmd.sunk | while | flops 68420608 | bytes 7505253 | solution.py:51
  201.0 1.3 constant_dynamic-slice_fusion.3
  202.3 0.2 copy.106
  202.5 0.3 fusion.90
  202.8 0.3 fusion.91
  203.1 0.2 copy.107
  203.4 0.4 fusion.92
  203.8 1.3 constant_dynamic-slice_fusion.3
  205.0 0.2 copy.106
  205.3 0.3 fusion.90
  205.6 0.3 fusion.91
  205.9 0.2 copy.107
  206.1 0.4 fusion.92
  206.5 1.3 constant_dynamic-slice_fusion.3
  207.8 0.2 copy.106
  208.0 0.3 fusion.90
  208.3 0.3 fusion.91
  208.7 0.2 copy.107
  208.9 0.4 fusion.92
  209.3 1.3 constant_dynamic-slice_fusion.3
  210.5 0.2 copy.106
  210.8 0.3 fusion.90
  211.1 0.3 fusion.91
  211.4 0.2 copy.107
  211.6 0.4 fusion.92
  212.0 0.1 broadcast_divide_fusion
  212.3 0.5 convolution_convert_fusion
  212.8 1.5 reshape.214
  214.3 9.5 %all-to-all-start.1 = ((bf16[64,2,4096]{2,1,0:T(2,128)(2,1)}), bf16[64,2,4096]{2,1,0:T(2,128)(2,1)S(1)}, u32[]{:S(2)}, u32[]{:S(2)}) async-start(bf16[64,2,4096]{2,1,0:T(2,128)(2,1)} %reshape.214), calls=%async_computation.1 | async-start | bytes 2097152 | tf_op jit(solution)/shard_map/all_to_all | solution.py:143
  223.8 1.5 reshape.204
  225.3 0.4 fusion.21
  225.7 23.5 %all-to-all-done.1 = bf16[64,2,4096]{2,1,0:T(2,128)(2,1)S(1)} async-done(((bf16[64,2,4096]{2,1,0:T(2,128)(2,1)}), bf16[64,2,4096]{2,1,0:T(2,128)(2,1)S(1)}, u32[]{:S(2)}, u32[]{:S(2)}) %all-to-all-start.1) | async-done | bytes 1048608 | tf_op jit(solution)/shard_map/all_to_all | solution.py:143
  249.2 1.2 multiply_reduce_fusion.1
  250.4 0.1 rsqrt.13
  250.5 0.3 reshape.217
  250.9 0.5 multiply_reduce_fusion
  251.4 0.7 copy-done.2
  252.1 1.7 add_convert_fusion
  253.8 2.5 reshape.215
  256.3 6.9 %all-to-all-start.2 = ((bf16[64,2,4096]{2,1,0:T(2,128)(2,1)}), bf16[64,2,4096]{2,1,0:T(2,128)(2,1)}, u32[]{:S(2)}, u32[]{:S(2)}) async-start(bf16[64,2,4096]{2,1,0:T(2,128)(2,1)} %reshape.215), calls=%async_computation.2 | async-start | bytes 2097152 | tf_op jit(solution)/shard_map/all_to_all | solution.py:167
  263.2 0.2 all-reduce.3.cloned.1.call-start
  263.4 2.4 multiply_convert_fusion
  265.8 2.3 convert_element_type.95
  268.2 1.0 fusion.12
  269.1 2.8 fusion.13
  271.9 71.4 %all-reduce.3.cloned.1.call-done = (bf16[1,16,4096]{2,1,0:T(8,128)(2,1)}, bf16[1,16,4096]{2,1,0:T(8,128)(2,1)}) async-done(((bf16[1,16,4096]{2,1,0:T(8,128)(2,1)}, bf16[1,16,4096]{2,1,0:T(8,128)(2,1)}), (bf16[1,16,4096]{2,1,0:T(8,128)(2,1)}, bf16[1,16,4096]{2,1,0:T(8,128)(2,1)})) %all-reduce.3.cloned.1.call-update) | async-done | bytes 262160 | tf_op jit(solution)/shard_map/psum | solution.py:174
  343.4 1.6 broadcast_in_dim.108
  345.0 1.6 broadcast_in_dim.110
  346.6 1.5 reshape.216
  348.1 1.0 convolution_convert_fusion.3
  (57 shorter events, 1.0 us)
Async XLA Ops:
  7.2 243.7 %copy-start = (bf16[1,16,4096]{2,1,0:T(8,128)(2,1)S(1)}, bf16[1,16,4096]{2,1,0:T(8,128)(2,1)}, u32[]{:S(2)}) copy-start(bf16[1,16,4096]{2,1,0:T(8,128)(2,1)} %param.20) | copy-start | bytes 393220
  7.2 6.2 %copy-start.9 = (s32[16,1]{0,1:T(1,128)S(1)}, s32[16,1]{0,1:T(1,128)}, u32[]{:S(2)}) copy-start(s32[16,1]{0,1:T(1,128)} %param.18) | copy-start | bytes 196
  7.2 6.4 %copy-start.8 = (bf16[16,4096]{1,0:T(8,128)(2,1)S(1)}, bf16[16,4096]{1,0:T(8,128)(2,1)}, u32[]{:S(2)}) copy-start(bf16[16,4096]{1,0:T(8,128)(2,1)} %param.19) | copy-start | bytes 393220
  7.2 109.7 %all-gather.3.cloned.1.call-start = ((), (), s32[]{:S(2)}) async-start(), calls=%async_computation.3 | async-start | bytes 2129920 | tf_op jit(solution)/shard_map/all_gather | solution.py:92
  10.7 190.3 %all-gather.5.cloned.1.call-start = ((), (), s32[]{:S(2)}) async-start(), calls=%async_computation.4 | async-start | bytes 2129920 | tf_op jit(solution)/shard_map/all_gather | solution.py:93
  14.0 19.1 %copy-start.7 = (bf16[16,4096]{1,0:T(8,128)(2,1)S(1)}, bf16[16,4096]{1,0:T(8,128)(2,1)}, u32[]{:S(2)}) copy-start(bf16[16,4096]{1,0:T(8,128)(2,1)} %param.12) | copy-start | bytes 393220
  14.1 19.2 %copy-start.4 = (bf16[256,1024]{1,0:T(8,128)(2,1)S(1)}, bf16[256,1024]{1,0:T(8,128)(2,1)}, u32[]{:S(2)}) copy-start(bf16[256,1024]{1,0:T(8,128)(2,1)} %param.13) | copy-start | bytes 1572868
  15.6 17.8 %copy-start.5 = (bf16[256,1024]{1,0:T(8,128)(2,1)S(1)}, bf16[256,1024]{1,0:T(8,128)(2,1)}, u32[]{:S(2)}) copy-start(bf16[256,1024]{1,0:T(8,128)(2,1)} %param.14) | copy-start | bytes 1572868
  15.6 198.7 %all-to-all-start = ((bf16[64,2,4096]{2,1,0:T(2,128)(2,1)}), bf16[64,2,4096]{2,1,0:T(2,128)(2,1)}, u32[]{:S(2)}, u32[]{:S(2)}) async-start(bf16[64,2,4096]{2,1,0:T(2,128)(2,1)} %reshape.203), calls=%async_computation | async-start | bytes 2097152 | tf_op jit(solution)/shard_map/all_to_all | solution.py:144
  214.3 11.0 %copy-start.6 = (bf16[1,16,4096]{2,1,0:T(8,128)(2,1)S(1)}, bf16[1,16,4096]{2,1,0:T(8,128)(2,1)}, u32[]{:S(2)}) copy-start(bf16[1,16,4096]{2,1,0:T(8,128)(2,1)} %param.21) | copy-start | bytes 393220
  214.3 34.9 %all-to-all-start.1 = ((bf16[64,2,4096]{2,1,0:T(2,128)(2,1)}), bf16[64,2,4096]{2,1,0:T(2,128)(2,1)S(1)}, u32[]{:S(2)}, u32[]{:S(2)}) async-start(bf16[64,2,4096]{2,1,0:T(2,128)(2,1)} %reshape.214), calls=%async_computation.1 | async-start | bytes 2097152 | tf_op jit(solution)/shard_map/all_to_all | solution.py:143
  225.3 25.1 %copy-start.1 = (bf16[128,4096]{1,0:T(8,128)(2,1)}, bf16[128,4096]{1,0:T(8,128)(2,1)S(1)}, u32[]{:S(2)}) copy-start(bf16[128,4096]{1,0:T(8,128)(2,1)S(1)} %reshape.204) | copy-start | bytes 3145732
  250.9 1.2 copy-start.2
  256.3 90.3 %all-to-all-start.2 = ((bf16[64,2,4096]{2,1,0:T(2,128)(2,1)}), bf16[64,2,4096]{2,1,0:T(2,128)(2,1)}, u32[]{:S(2)}, u32[]{:S(2)}) async-start(bf16[64,2,4096]{2,1,0:T(2,128)(2,1)} %reshape.215), calls=%async_computation.2 | async-start | bytes 2097152 | tf_op jit(solution)/shard_map/all_to_all | solution.py:167
  263.2 80.2 %all-reduce.3.cloned.1.call-start = ((), (), s32[]{:S(2)}) async-start(), calls=%async_computation.5 | async-start | bytes 524288 | tf_op jit(solution)/shard_map/psum | solution.py:174
  265.8 3.3 copy-start.3
Sparse Core Ops, SparseCore 0:
  11.6 105.2 all-gather.2
  120.5 80.5 all-gather.4
  272.1 71.2 all-reduce.2
where the time goes:
time: 356 us
  waiting for transfers between devices  261 us (73%)
  starting transfers between devices  33.6 us (9%)
  local copies, waits for them, and re-layouts  20.5 us (6%)
  between operations  15.3 us (4%)
  matrix products  14.1 us (4%)
  other arithmetic  10.5 us (3%)
    all_gather x1, waiting for transfers between devices, attend(): lax.all_gather(short_vals, 'ctx', axis=0, tiled=True)  84.1 us
    all_gather x1, waiting for transfers between devices, attend(): lax.all_gather(short_keys, 'ctx', axis=0, tiled=True)  82.2 us
    psum x1, waiting for transfers between devices, shards(): lax.psum(grad_a.astype(jnp.bfloat16), 'dp').astype(jnp.float32)  71.4 us
    all_to_all x1, waiting for transfers between devices, shards(): lax.all_to_all(packed(attn), 'ctx', split_axis=0, concat_axis=0, tiled=True)  23.5 us
    all_to_all x1, starting transfers between devices, shards(): lax.all_to_all(packed(dy), 'ctx', split_axis=0, concat_axis=0, tiled=True)  16.9 us
    all_to_all x1, starting transfers between devices, shards(): lax.all_to_all(packed(attn), 'ctx', split_axis=0, concat_axis=0, tiled=True)  9.51 us
  transfers between devices with their start and end apart: 6, of which 4 were waited for; matrix products, arithmetic and copies ran while one was open for 9% of the time, Pallas kernels for 0%

commit v1 on v0

--- a/solution.py
+++ b/solution.py
@@ -171,7 +171,7 @@
         place, returned.reshape(count * cap, model), along, preferred_element_type=jnp.float32
     ).astype(jnp.bfloat16)
     grad_a, grad_b = (
-        lax.psum(grad_a.astype(jnp.bfloat16), "dp").astype(jnp.float32),
+        jnp.sum(lax.all_gather(grad_a.astype(jnp.bfloat16), "dp"), axis=0).astype(jnp.float32),
         lax.psum(grad_b.astype(jnp.bfloat16), "dp").astype(jnp.float32),
     )
     return (grad_rows, grad_a[None], grad_b[None])

time: 356 us -> 367 us (1.031)
  the two profiles are of different devices: /device:TPU:8 before, /device:TPU:1 now
where the time goes in v1:
time: 367 us; the launch traced here: 366 us
  waiting for transfers between devices  266 us (72%)
  starting transfers between devices  38.8 us (11%)
  local copies, waits for them, and re-layouts  18.8 us (5%)
  between operations  15.4 us (4%)
  matrix products  15.3 us (4%)
  other arithmetic  11.5 us (3%)
    all_gather x1, waiting for transfers between devices, attend(): lax.all_gather(short_vals, 'ctx', axis=0, tiled=True)  84.1 us
    all_gather x1, waiting for transfers between devices, attend(): lax.all_gather(short_keys, 'ctx', axis=0, tiled=True)  78.3 us
    psum x1, waiting for transfers between devices, shards(): lax.psum(grad_b.astype(jnp.bfloat16), 'dp').astype(jnp.float32)  51.7 us
    all_gather x1, waiting for transfers between devices, shards(): lax.all_gather(grad_a.astype(jnp.bfloat16), 'dp')  31 us
    all_to_all x1, waiting for transfers between devices, shards(): lax.all_to_all(packed(attn), 'ctx', split_axis=0, concat_axis=0, tiled=True)  20.9 us
    all_to_all x1, starting transfers between devices, shards(): lax.all_to_all(packed(dy), 'ctx', split_axis=0, concat_axis=0, tiled=True)  17.3 us
    all_to_all x1, starting transfers between devices, shards(): lax.all_to_all(d_rows.reshape(count, cap, model), 'ctx', split_axis=0, co...  12.8 us
    all_to_all x1, starting transfers between devices, shards(): lax.all_to_all(packed(attn), 'ctx', split_axis=0, concat_axis=0, tiled=True)  8.4 us
  transfers between devices with their start and end apart: 7, of which 5 were waited for; matrix products, arithmetic and copies ran while one was open for 8% of the time, Pallas kernels for 0%

profile of v1, /device:TPU:1, one launch (start us, length us, event | category | flops | bytes accessed | tf_op | source)
XLA Modules:
  0.0 366.3 jit_solution(4329205452880708468)
XLA Ops:
  7.2 1.5 fusion.60
  8.8 1.3 fusion.18
  10.1 0.6 copy.103
  10.8 1.3 fusion.19
  12.0 0.6 copy.102
  13.6 0.5 convolution_convert_fusion.1
  14.1 1.5 reshape.212
  15.6 17.3 %all-to-all-start = ((bf16[64,2,4096]{2,1,0:T(2,128)(2,1)}), bf16[64,2,4096]{2,1,0:T(2,128)(2,1)S(1)}, u32[]{:S(2)}, u32[]{:S(2)}) async-start(bf16[64,2,4096]{2,1,0:T(2,128)(2,1)} %reshape.212), calls=%async_computation | async-start | bytes 2097152 | tf_op jit(solution)/shard_map/all_to_all | solution.py:144
  34.0 0.4 fusion.59
  34.4 0.3 fusion.31
  34.7 0.3 fusion.15
  35.0 78.3 %all-gather.5.cloned.1.call-done = bf16[1024,1024]{1,0:T(8,128)(2,1)} async-done(((bf16[16,1024]{1,0:T(8,128)(2,1)}), bf16[1024,1024]{1,0:T(8,128)(2,1)}) %all-gather.5.cloned.1.call-update) | async-done | bytes 2097168 | tf_op jit(solution)/shard_map/all_gather | solution.py:92
  113.3 84.1 %all-gather.7.cloned.1.call-done = bf16[1024,1024]{1,0:T(8,128)(2,1)} async-done(((bf16[16,1024]{1,0:T(8,128)(2,1)}), bf16[1024,1024]{1,0:T(8,128)(2,1)}) %all-gather.7.cloned.1.call-update) | async-done | bytes 2097168 | tf_op jit(solution)/shard_map/all_gather | solution.py:93
  197.4 11.0 %while.14 = (s32[]{:T(128)}, f32[16,8,4]{0,2,1:T(4,128)S(1)}, f32[16,8,4]{0,2,1:T(4,128)S(1)}, f32[16,8,4,128]{3,0,2,1:T(8,128)S(1)}, pred[4,1,256]{2,1,0:T(4,12...) while((s32[]{:T(128)}, f32[16,8,4]{0,2,1:T(4,128)S(1)}, ...), condition=%wide.region_8.9_spmd, body=%wide.region_5.8_spmd.sunk | while | flops 68420608 | bytes 7505253 | solution.py:51
  197.4 1.3 constant_dynamic-slice_fusion.3
  198.7 0.2 copy.106
  198.9 0.3 fusion.89
  199.2 0.3 fusion.90
  199.6 0.2 copy.107
  199.8 0.4 fusion.91
  200.2 1.3 constant_dynamic-slice_fusion.3
  201.4 0.2 copy.106
  201.7 0.3 fusion.89
  202.0 0.3 fusion.90
  202.3 0.2 copy.107
  202.5 0.4 fusion.91
  202.9 1.3 constant_dynamic-slice_fusion.3
  204.2 0.2 copy.106
  204.4 0.3 fusion.89
  204.8 0.3 fusion.90
  205.1 0.2 copy.107
  205.3 0.4 fusion.91
  205.7 1.3 constant_dynamic-slice_fusion.3
  207.0 0.2 copy.106
  207.2 0.3 fusion.89
  207.5 0.3 fusion.90
  207.8 0.2 copy.107
  208.0 0.4 fusion.91
  208.7 0.5 convolution_convert_fusion
  209.2 1.5 reshape.223
  210.7 1.0 copy-done.3
  211.7 8.4 %all-to-all-start.1 = ((bf16[64,2,4096]{2,1,0:T(2,128)(2,1)}), bf16[64,2,4096]{2,1,0:T(2,128)(2,1)S(1)}, u32[]{:S(2)}, u32[]{:S(2)}) async-start(bf16[64,2,4096]{2,1,0:T(2,128)(2,1)} %reshape.223), calls=%async_computation.1 | async-start | bytes 2097152 | tf_op jit(solution)/shard_map/all_to_all | solution.py:143
  220.2 1.5 reshape.213
  221.7 0.4 fusion.20
  222.1 20.9 %all-to-all-done.1 = bf16[64,2,4096]{2,1,0:T(2,128)(2,1)S(1)} async-done(((bf16[64,2,4096]{2,1,0:T(2,128)(2,1)}), bf16[64,2,4096]{2,1,0:T(2,128)(2,1)S(1)}, u32[]{:S(2)}, u32[]{:S(2)}) %all-to-all-start.1) | async-done | bytes 1048608 | tf_op jit(solution)/shard_map/all_to_all | solution.py:143
  243.0 1.2 multiply_reduce_fusion.1
  244.3 1.4 multiply_convert_fusion
  245.8 1.2 convert_element_type.111
  247.0 0.3 reshape.226
  247.3 1.0 convolution_convert_fusion.2
  248.3 1.8 multiply_reduce_fusion
  250.1 2.8 fusion.12
  252.9 0.2 all-gather.9.cloned.1.call-start
  253.2 0.3 all-gather.9.cloned.1.call-update
  253.5 3.2 add_convert_fusion
  256.7 2.5 reshape.224
  259.2 12.8 %all-to-all-start.2 = ((bf16[64,2,4096]{2,1,0:T(2,128)(2,1)}), bf16[64,2,4096]{2,1,0:T(2,128)(2,1)S(1)}, u32[]{:S(2)}, u32[]{:S(2)}) async-start(bf16[64,2,4096]{2,1,0:T(2,128)(2,1)} %reshape.224), calls=%async_computation.2 | async-start | bytes 2097152 | tf_op jit(solution)/shard_map/all_to_all | solution.py:167
  272.0 51.7 %all-reduce.2.cloned.1.call-done = bf16[1,16,4096]{2,1,0:T(8,128)(2,1)} async-done(((bf16[1,16,4096]{2,1,0:T(8,128)(2,1)}), bf16[1,16,4096]{2,1,0:T(8,128)(2,1)}) %all-reduce.2.cloned.1.call-update) | async-done | bytes 131088 | tf_op jit(solution)/shard_map/psum | solution.py:175
  323.6 1.6 broadcast_in_dim.103
  325.3 31.0 %all-gather.9.cloned.1.call-done = bf16[128,4096]{1,0:T(8,128)(2,1)} async-done(((bf16[16,4096]{1,0:T(8,128)(2,1)}), bf16[128,4096]{1,0:T(8,128)(2,1)}) %all-gather.9.cloned.1.call-update) | async-done | bytes 1048592 | tf_op jit(solution)/shard_map/all_gather | solution.py:174
  356.2 1.4 reduce_sum.71
  357.6 0.7 bitcast_convert_fusion
  358.3 0.4 reshape.225
  358.8 1.0 convolution_convert_fusion.3
  (61 shorter events, 1.5 us)
Async XLA Ops:
  7.2 241.1 %copy-start = (bf16[1,16,4096]{2,1,0:T(8,128)(2,1)S(1)}, bf16[1,16,4096]{2,1,0:T(8,128)(2,1)}, u32[]{:S(2)}) copy-start(bf16[1,16,4096]{2,1,0:T(8,128)(2,1)} %param.20) | copy-start | bytes 393220
  7.2 6.2 %copy-start.9 = (s32[16,1]{0,1:T(1,128)S(1)}, s32[16,1]{0,1:T(1,128)}, u32[]{:S(2)}) copy-start(s32[16,1]{0,1:T(1,128)} %param.18) | copy-start | bytes 196
  7.2 6.4 %copy-start.8 = (bf16[16,4096]{1,0:T(8,128)(2,1)S(1)}, bf16[16,4096]{1,0:T(8,128)(2,1)}, u32[]{:S(2)}) copy-start(bf16[16,4096]{1,0:T(8,128)(2,1)} %param.19) | copy-start | bytes 393220
  7.2 106.1 %all-gather.5.cloned.1.call-start = ((), (), s32[]{:S(2)}) async-start(), calls=%async_computation.3 | async-start | bytes 2129920 | tf_op jit(solution)/shard_map/all_gather | solution.py:92
  10.7 186.7 %all-gather.7.cloned.1.call-start = ((), (), s32[]{:S(2)}) async-start(), calls=%async_computation.4 | async-start | bytes 2129920 | tf_op jit(solution)/shard_map/all_gather | solution.py:93
  14.0 19.5 %copy-start.7 = (bf16[16,4096]{1,0:T(8,128)(2,1)S(1)}, bf16[16,4096]{1,0:T(8,128)(2,1)}, u32[]{:S(2)}) copy-start(bf16[16,4096]{1,0:T(8,128)(2,1)} %param.12) | copy-start | bytes 393220
  14.1 19.5 %copy-start.4 = (bf16[256,1024]{1,0:T(8,128)(2,1)S(1)}, bf16[256,1024]{1,0:T(8,128)(2,1)}, u32[]{:S(2)}) copy-start(bf16[256,1024]{1,0:T(8,128)(2,1)} %param.13) | copy-start | bytes 1572868
  15.6 18.1 %copy-start.5 = (bf16[256,1024]{1,0:T(8,128)(2,1)S(1)}, bf16[256,1024]{1,0:T(8,128)(2,1)}, u32[]{:S(2)}) copy-start(bf16[256,1024]{1,0:T(8,128)(2,1)} %param.14) | copy-start | bytes 1572868
  15.6 195.1 %all-to-all-start = ((bf16[64,2,4096]{2,1,0:T(2,128)(2,1)}), bf16[64,2,4096]{2,1,0:T(2,128)(2,1)S(1)}, u32[]{:S(2)}, u32[]{:S(2)}) async-start(bf16[64,2,4096]{2,1,0:T(2,128)(2,1)} %reshape.212), calls=%async_computation | async-start | bytes 2097152 | tf_op jit(solution)/shard_map/all_to_all | solution.py:144
  210.7 11.0 %copy-start.6 = (bf16[1,16,4096]{2,1,0:T(8,128)(2,1)S(1)}, bf16[1,16,4096]{2,1,0:T(8,128)(2,1)}, u32[]{:S(2)}) copy-start(bf16[1,16,4096]{2,1,0:T(8,128)(2,1)} %param.21) | copy-start | bytes 393220
  210.7 1.0 copy-start.3
  211.7 31.2 %all-to-all-start.1 = ((bf16[64,2,4096]{2,1,0:T(2,128)(2,1)}), bf16[64,2,4096]{2,1,0:T(2,128)(2,1)S(1)}, u32[]{:S(2)}, u32[]{:S(2)}) async-start(bf16[64,2,4096]{2,1,0:T(2,128)(2,1)} %reshape.223), calls=%async_computation.1 | async-start | bytes 2097152 | tf_op jit(solution)/shard_map/all_to_all | solution.py:143
  220.1 103.5 %all-reduce.2.cloned.1.call-start = ((), (), s32[]{:S(2)}) async-start(), calls=%async_computation.5 | async-start | bytes 262144 | tf_op jit(solution)/shard_map/psum | solution.py:175
  221.7 24.1 %copy-start.1 = (bf16[128,4096]{1,0:T(8,128)(2,1)}, bf16[128,4096]{1,0:T(8,128)(2,1)S(1)}, u32[]{:S(2)}) copy-start(bf16[128,4096]{1,0:T(8,128)(2,1)S(1)} %reshape.213) | copy-start | bytes 3145732
  248.3 1.8 copy-start.2
  252.9 103.3 %all-gather.9.cloned.1.call-start = ((), (), s32[]{:S(2)}) async-start(), calls=%async_computation.6 | async-start | bytes 1179648 | tf_op jit(solution)/shard_map/all_gather | solution.py:174
  259.2 99.1 %all-to-all-start.2 = ((bf16[64,2,4096]{2,1,0:T(2,128)(2,1)}), bf16[64,2,4096]{2,1,0:T(2,128)(2,1)S(1)}, u32[]{:S(2)}, u32[]{:S(2)}) async-start(bf16[64,2,4096]{2,1,0:T(2,128)(2,1)} %reshape.224), calls=%async_computation.2 | async-start | bytes 2097152 | tf_op jit(solution)/shard_map/all_to_all | solution.py:167
Sparse Core Ops, SparseCore 0:
  11.6 101.6 all-gather.4
  116.9 80.5 all-gather.6
  253.0 70.5 all-reduce.1
  326.5 29.7 all-gather.8
